TPU v7x, 128 devices: a whole 4x4x4 slice. The times are simulated.
128 devices in a mesh: row: 4 (over y), col: 32 (over z, x, core).
Axes of the slice: x: 4, y: 4, z: 4, core: 2. Of those that a mesh axis runs over, the one named last changes fastest.
Arguments:
- tokens: bfloat16 [768, 8192], P('col', 'row'), may hold values from -6 to 6
- gate_weight: bfloat16 [8192, 28672], P('row', 'col'), may hold values from -0.0625 to 0.0625
- up_weight: bfloat16 [8192, 28672], P('row', 'col'), may hold values from -0.0625 to 0.0625
- down_weight: bfloat16 [28672, 8192], P('col', 'row'), may hold values from -0.03125 to 0.03125
- mask_gate: int32 [128, 448], P('row', 'col'), may hold values from 0 to 1, as said below
- mask_up: int32 [128, 448], P('row', 'col'), may hold values from 0 to 1, as said below
- mask_down: int32 [448, 128], P('col', 'row'), may hold values from 0 to 1, as said below
- cotangent: bfloat16 [768, 8192], P('col', 'row'), may hold values from -1.5 to 1.5
Outputs:
- output: bfloat16 [768, 8192], P('col', 'row')
- grad_input: bfloat16 [768, 8192], P('col', 'row')
- grad_gate: bfloat16 [8192, 28672], P('row', 'col')
- grad_up: bfloat16 [8192, 28672], P('row', 'col')
- grad_down: bfloat16 [28672, 8192], P('col', 'row')
Inputs may be any that keep to these rules, and one draw needn't show every extreme that they name: `mask_gate`: 1 where a 64 x 64 block of the weight is kept, 0 where it is pruned. `mask_up`: 1 where a 64 x 64 block of the weight is kept, 0 where it is pruned. `mask_down`: 1 where a 64 x 64 block of the weight is kept, 0 where it is pruned.
All inputs are finite; a program needn't handle non-finite values.
Results may differ from a plain program's by a relative error of at most 0.006.
Values may be sent and summed in bfloat16 or wider, within the bound.
No kernel may reach another device: no remote copies, remote signals or barrier semaphores. Data moves between devices by JAX's collectives and lax.ppermute only.
A program may use at most 128 MiB of HBM per device.

v0:
```python
import jax
import jax.numpy as jnp
from jax import lax
from jax.sharding import PartitionSpec as P

BLOCK = 64


def expand(mask):
    return jnp.repeat(jnp.repeat(mask, BLOCK, 0), BLOCK, 1).astype(jnp.bfloat16)


def contract_last(left, right):
    return lax.dot_general(
        left, right, (((1,), (1,)), ((), ())), preferred_element_type=jnp.float32
    )


def contract_first(left, right):
    return lax.dot_general(
        left, right, (((0,), (0,)), ((), ())), preferred_element_type=jnp.float32
    )


def backward_gates(dhid, gate, up):
    sigma = jax.nn.sigmoid(gate)
    dgate = (dhid * up * sigma * (1.0 + gate * (1.0 - sigma))).astype(jnp.bfloat16)
    dup = (dhid * gate * sigma).astype(jnp.bfloat16)
    return (dgate, dup)


def body(tokens, gate_weight, up_weight, down_weight, mask_gate, mask_up, mask_down, cotangent):
    keep_gate = expand(mask_gate)
    keep_up = expand(mask_up)
    keep_down = expand(mask_down)
    w_gate = gate_weight * keep_gate
    w_up = up_weight * keep_up
    w_down = down_weight * keep_down
    width = w_gate.shape[1]
    panel = lax.all_gather(tokens, "col", axis=0, tiled=True)
    stacked = jnp.concatenate([w_gate, w_up], axis=1)
    partial_both = jnp.dot(panel, stacked, preferred_element_type=jnp.float32)
    summed = lax.psum(partial_both, "row")
    gate = summed[:, :width]
    up = summed[:, width:]
    hidden = (jax.nn.silu(gate) * up).astype(jnp.bfloat16)
    output = lax.psum_scatter(
        jnp.dot(hidden, w_down, preferred_element_type=jnp.float32),
        "col",
        scatter_dimension=0,
        tiled=True,
    ).astype(jnp.bfloat16)
    cot_panel = lax.all_gather(cotangent, "col", axis=0, tiled=True)
    partial_dhid = contract_last(cot_panel, w_down)
    dhid = lax.psum(partial_dhid, "row")
    dgate, dup = backward_gates(dhid, gate, up)
    grad_down = (contract_first(hidden, cot_panel) * keep_down).astype(jnp.bfloat16)
    grad_gate = (contract_first(panel, dgate) * keep_gate).astype(jnp.bfloat16)
    grad_up = (contract_first(panel, dup) * keep_up).astype(jnp.bfloat16)
    grad_input = lax.psum_scatter(
        contract_last(dgate, w_gate) + contract_last(dup, w_up),
        "col",
        scatter_dimension=0,
        tiled=True,
    ).astype(jnp.bfloat16)
    return (output, grad_input, grad_gate, grad_up, grad_down)


def solution(mesh):
    return jax.shard_map(
        body,
        mesh=mesh,
        in_specs=(
            P("col", "row"),
            P("row", "col"),
            P("row", "col"),
            P("col", "row"),
            P("row", "col"),
            P("row", "col"),
            P("col", "row"),
            P("col", "row"),
        ),
        out_specs=(
            P("col", "row"),
            P("col", "row"),
            P("row", "col"),
            P("row", "col"),
            P("col", "row"),
        ),
        check_vma=False,
    )
```

profile of v0, /device:TPU:0, one launch (start us, length us, event | category | flops | bytes accessed | tf_op | source)
XLA Modules:
  0.0 472.1 jit_solution(7040883705480512886)
XLA Ops:
  7.2 0.0 all-gather.5.cloned.1.call-start
  7.2 0.7 all-gather.5.cloned.1.call-update
  7.9 0.0 all-gather.3.cloned.1.call-start
  7.9 0.7 all-gather.3.cloned.1.call-update
  8.6 0.0 all-reduce.3.cloned.1.call-start
  8.7 0.7 convert_element_type.66
  9.4 0.1 broadcast_in_dim.18
  9.5 0.1 convert_element_type.67
  9.7 0.7 convert_element_type.69
  10.4 0.1 broadcast_in_dim.20
  10.5 0.1 convert_element_type.70
  10.7 6.1 %copy.24 = bf16[2048,896]{0,1:T(8,128)(2,1)} copy(bf16[2048,896]{1,0:T(8,128)(2,1)} %param.9) | data formatting | bytes 7340032 | tf_op args[1]
  16.7 6.1 %copy.25 = bf16[2048,896]{0,1:T(8,128)(2,1)} copy(bf16[2048,896]{1,0:T(8,128)(2,1)} %param.10) | data formatting | bytes 7340032 | tf_op args[2]
  22.8 0.0 copy-done.5
  22.8 0.1 copy.26
  22.9 0.1 broadcast_in_dim.22
  23.0 0.1 convert_element_type.74
  23.2 6.1 %copy.27 = bf16[896,2048]{0,1:T(8,128)(2,1)} copy(bf16[896,2048]{1,0:T(8,128)(2,1)} %param.11) | data formatting | bytes 7340032 | tf_op args[3]
  29.2 4.4 bitcast_multiply_fusion.4
  33.7 0.0 copy-done
  33.7 1.2 copy-done.1
  34.8 3.6 bitcast_multiply_fusion.2
  38.4 19.5 %all-gather.5.cloned.1.call-done = bf16[768,2048]{1,0:T(8,128)(2,1)} async-done(((bf16[24,2048]{1,0:T(8,128)(2,1)}), bf16[768,2048]{1,0:T(8,128)(2,1)}) %all-gather.5.cloned.1.call-update) | async-done | bytes 3145744 | tf_op jit(solution)/shard_map/all_gather | solution.py:53
  57.9 7.6 %convolution_bitcast_fusion = f32[768,896]{0,1:T(8,128)} fusion(bf16[896,2048]{0,1:T(8,128)(2,1)} %bitcast_multiply_fusion.4, bf16[768,2048]{1,0:T(8,128)(2,1)} %all-gather.5.cloned.1.call-done), kind=kOutput, calls=%fused_computation.18 | convolution fusion | flops 2818572288 | bytes 9568256 | tf_op jit(solution)/shard_map/dot_general | solution.py:14
  65.5 39.1 %all-gather.3.cloned.1.call-done = bf16[768,2048]{1,0:T(8,128)(2,1)} async-done(((bf16[24,2048]{1,0:T(8,128)(2,1)}), bf16[768,2048]{1,0:T(8,128)(2,1)}) %all-gather.3.cloned.1.call-update) | async-done | bytes 3145744 | tf_op jit(solution)/shard_map/all_gather | solution.py:40
  104.7 12.3 %fusion.6 = f32[768,1792]{0,1:T(8,128)} fusion(bf16[768,2048]{1,0:T(8,128)(2,1)} %all-gather.3.cloned.1.call-done, bf16[2048,896]{0,1:T(8,128)(2,1)} %get-tuple-element.25, bf16[2048,896]{0,1:T(8,128)(2,1)} %get-tuple-element.26), kind=kOutput, calls=%fused_computation.11 | convolution fusion | flops 5651824640 | bytes 15990784 | tf_op jit(solution)/shard_map/dot_general | solution.py:42
  117.0 0.0 all-reduce.3.cloned.1.call-update
  117.0 0.2 reduce-scatter.5.cloned.1.call-start
  117.3 157.7 %all-reduce.3.cloned.1.call-done = (f32[768,1792]{0,1:T(8,128)}, f32[768,896]{0,1:T(8,128)}) async-done(((f32[768,1792]{0,1:T(8,128)}, f32[768,896]{0,1:T(8,128)}), (f32[768,1792]{0,1:T(8,128)}, f32[768,896]{0,1:T(8,128)})) %all-reduce.3.cloned.1.call-update) | async-done | bytes 8257552 | tf_op jit(solution)/shard_map/psum | solution.py:43
  274.9 4.3 multiply_convert_fusion.1
  279.3 0.1 copy-done.3
  279.4 3.5 fusion.11
  283.0 5.4 %convolution_add_fusion = f32[768,2048]{1,0:T(8,128)} fusion(f32[768,2048]{1,0:T(8,128)S(1)} %fusion.11, bf16[768,896]{0,1:T(8,128)(2,1)S(1)} %get-tuple-element.22, bf16[2048,896]{0,1:T(8,128)(2,1)S(1)} %copy-done.2), kind=kOutput, calls=%fused_computation.12 | convolution fusion | flops 2820145152 | bytes 17629184 | tf_op jit(solution)/shard_map/dot_general | solution.py:14
  288.3 0.0 reduce-scatter.5.cloned.1.call-update
  288.4 0.0 reduce-scatter.3.cloned.1.call-start
  288.4 7.4 %fusion.10 = f32[768,2048]{1,0:T(8,128)} fusion(bf16[768,896]{0,1:T(8,128)(2,1)S(1)} %get-tuple-element.24, bf16[896,2048]{0,1:T(8,128)(2,1)} %bitcast_multiply_fusion.4), kind=kOutput, calls=%fused_computation.20 | convolution fusion | flops 2818572288 | bytes 11337728 | tf_op jit(solution)/shard_map/dot_general | solution.py:48
  295.9 0.0 reduce-scatter.3.cloned.1.call-update
  295.9 2.1 broadcast_in_dim.23
  298.0 6.2 %copy.28 = bf16[896,2048]{1,0:T(8,128)(2,1)} copy(bf16[896,2048]{0,1:T(8,128)(2,1)} %bitcast.41) | data formatting | bytes 7340032 | tf_op jit(solution)/shard_map/convert_element_type | solution.py:10
  304.2 7.3 %fusion.5 = bf16[2048,896]{0,1:T(8,128)(2,1)} fusion(bf16[768,896]{0,1:T(8,128)(2,1)} %copy-done.4, bf16[768,2048]{1,0:T(8,128)(2,1)} %all-gather.3.cloned.1.call-done, bf16[2048,14]{0,1:T(8,128)(2,1)S(1)} %convert_element_type.67), kind=kOutput, calls=%fused_computation.7 | convolution fusion | flops 2824077312 | bytes 8249344 | tf_op jit(solution)/shard_map/dot_general | solution.py:20
  311.5 6.2 %copy.29 = bf16[2048,896]{1,0:T(8,128)(2,1)} copy(bf16[2048,896]{0,1:T(8,128)(2,1)} %fusion.5) | data formatting | bytes 7340032
  317.7 6.9 %fusion.4 = bf16[2048,896]{0,1:T(8,128)(2,1)} fusion(bf16[768,896]{0,1:T(8,128)(2,1)S(1)} %get-tuple-element.22, bf16[768,2048]{1,0:T(8,128)(2,1)} %all-gather.3.cloned.1.call-done, bf16[2048,14]{0,1:T(8,128)(2,1)S(1)} %convert_element_type.70), kind=kOutput, calls=%fused_computation.5 | convolution fusion | flops 2824077312 | bytes 8249344 | tf_op jit(solution)/shard_map/dot_general | solution.py:20
  324.6 6.1 %copy.30 = bf16[2048,896]{1,0:T(8,128)(2,1)} copy(bf16[2048,896]{0,1:T(8,128)(2,1)} %fusion.4) | data formatting | bytes 7340032
  330.6 6.9 %multiply_convert_fusion = bf16[896,2048]{1,0:T(8,128)(2,1)} fusion(bf16[896,2048]{1,0:T(8,128)(2,1)} %copy.28, bf16[768,896]{0,1:T(8,128)(2,1)S(1)} %get-tuple-element.24, bf16[768,2048]{1,0:T(8,128)(2,1)} %all-gather.5.cloned.1.call-done), kind=kOutput, calls=%fused_computation.8 | convolution fusion | flops 2824077312 | bytes 11862016 | tf_op jit(solution)/shard_map/dot_general | solution.py:20
  337.5 37.2 %reduce-scatter.5.cloned.1.call-done = f32[24,2048]{1,0:T(8,128)} async-done(((f32[768,2048]{1,0:T(8,128)}), f32[24,2048]{1,0:T(8,128)}) %reduce-scatter.5.cloned.1.call-update) | async-done | bytes 196624 | tf_op jit(solution)/shard_map/reduce_scatter | solution.py:60
  374.8 1.6 convert_element_type.79
  376.3 87.7 %reduce-scatter.3.cloned.1.call-done = f32[24,2048]{1,0:T(8,128)} async-done(((f32[768,2048]{1,0:T(8,128)}), f32[24,2048]{1,0:T(8,128)}) %reduce-scatter.3.cloned.1.call-update) | async-done | bytes 196624 | tf_op jit(solution)/shard_map/reduce_scatter | solution.py:47
  464.0 1.6 convert_element_type.76
  (9 shorter events, 0.0 us)
Async XLA Ops:
  7.2 50.8 %all-gather.5.cloned.1.call-start = ((), (), s32[]{:S(2)}) async-start(), calls=%async_computation.4 | async-start | bytes 3244032 | tf_op jit(solution)/shard_map/all_gather | solution.py:53
  7.9 96.8 %all-gather.3.cloned.1.call-start = ((), (), s32[]{:S(2)}) async-start(), calls=%async_computation.2 | async-start | bytes 3244032 | tf_op jit(solution)/shard_map/all_gather | solution.py:40
  8.6 266.3 %all-reduce.3.cloned.1.call-start = ((), (), s32[]{:S(2)}) async-start(), calls=%async_computation.6 | async-start | bytes 16515072 | tf_op jit(solution)/shard_map/psum | solution.py:43
  16.7 6.1 %copy-start.5 = (s32[14,32]{1,0:T(8,128)S(1)}, s32[14,32]{1,0:T(8,128)}, u32[]{:S(2)}) copy-start(s32[14,32]{1,0:T(8,128)} %param.14) | copy-start | bytes 5380
  29.2 4.4 copy-start
  29.2 5.6 %copy-start.1 = (bf16[2048,896]{0,1:T(8,128)(2,1)S(1)}, bf16[2048,896]{0,1:T(8,128)(2,1)}, u32[]{:S(2)}) copy-start(bf16[2048,896]{0,1:T(8,128)(2,1)} %copy.25) | copy-start | bytes 11010052
  117.0 257.7 %reduce-scatter.5.cloned.1.call-start = ((), (), s32[]{:S(2)}) async-start(), calls=%async_computation.5 | async-start | bytes 6488064 | tf_op jit(solution)/shard_map/reduce_scatter | solution.py:60
  274.9 4.5 copy-start.3
  279.2 3.7 copy-start.4
  279.4 3.5 copy-start.2
  288.4 175.6 %reduce-scatter.3.cloned.1.call-start = ((), (), s32[]{:S(2)}) async-start(), calls=%async_computation.3 | async-start | bytes 6488064 | tf_op jit(solution)/shard_map/reduce_scatter | solution.py:47
Sparse Core Ops, SparseCore 0:
  10.3 47.6 all-gather.4
  60.2 44.4 all-gather.2
  117.2 157.7 all-reduce.2
  288.5 86.2 reduce-scatter.4
  378.3 85.6 reduce-scatter.2
where the time goes:
time: 473 us; the launch traced here: 472 us
  waiting for transfers between devices  343 us (73%)
  matrix products  57.4 us (12%)
  local copies, waits for them, and re-layouts  40.9 us (9%)
  other arithmetic  16.9 us (4%)
  between operations  13.9 us (3%)
    psum x1, waiting for transfers between devices, body(): summed = lax.psum(partial_both, 'row')  158 us
    reduce_scatter x1, waiting for transfers between devices, body(): lax.psum_scatter(jnp.dot(hidden, w_down, preferred_element_type=jnp.float...  87.7 us
    all_gather x1, waiting for transfers between devices, body(): panel = lax.all_gather(tokens, 'col', axis=0, tiled=True)  39.1 us
    reduce_scatter x1, waiting for transfers between devices, body(): lax.psum_scatter(contract_last(dgate, w_gate) + contract_last(dup, w_up),...  37.2 us
    unnamed x17, local copies, waits for them, and re-layouts  31.7 us
    dot_general x3, matrix products, contract_first(): lax.dot_general(left, right, (((0,), (0,)), ((), ())), preferred_element_...  21.1 us
    all_gather x1, waiting for transfers between devices, body(): cot_panel = lax.all_gather(cotangent, 'col', axis=0, tiled=True)  19.5 us
    dot_general x3, matrix products, contract_last(): lax.dot_general(left, right, (((1,), (1,)), ((), ())), preferred_element_...  16.5 us
  transfers between devices with their start and end apart: 5, of which 5 were waited for; matrix products, arithmetic and copies ran while one was open for 18% of the time, Pallas kernels for 0%

commit v1 on v0

--- a/solution.py
+++ b/solution.py
@@ -50,7 +50,9 @@
         scatter_dimension=0,
         tiled=True,
     ).astype(jnp.bfloat16)
-    cot_panel = lax.all_gather(cotangent, "col", axis=0, tiled=True)
+    cot_panel = jnp.concatenate(
+        lax.all_to_all(jnp.stack([cotangent] * lax.axis_size("col")), "col", 0, 0), axis=0
+    )
     partial_dhid = contract_last(cot_panel, w_down)
     dhid = lax.psum(partial_dhid, "row")
     dgate, dup = backward_gates(dhid, gate, up)

time: 473 us -> 451 us (0.953)
  waiting for transfers between devices: 343 us -> 309 us
  starting transfers between devices: 0.38 us -> 8.72 us
    all_gather x1, waiting for transfers between devices: 39.1 us -> 12.5 us  [body(): panel = lax.all_gather(tokens, 'col', axis=0, tiled=True)]
    all_gather x1 -> x0, waiting for transfers between devices: 19.5 us -> none  [body(): cot_panel = lax.all_gather(cotangent, 'col', axis=0, tiled=True)]
    all_to_all x0 -> x1, waiting for transfers between devices: none -> 14.4 us  [body(): lax.all_to_all(jnp.stack([cotangent] * lax.axis_size('col')), 'col', 0, 0)]
    all_to_all x0 -> x1, starting transfers between devices: none -> 8.38 us  [body(): lax.all_to_all(jnp.stack([cotangent] * lax.axis_size('col')), 'col', 0, 0)]
    unnamed x17 -> x23, local copies, waits for them, and re-layouts: 31.7 us -> 31.7 us
  transfers between devices with their start and end apart: 5 -> 5, of which waited for: 5 -> 5; matrix products, arithmetic and copies ran while one was open for 18% -> 20% of each run, Pallas kernels for 0% -> 0%
where the time goes in v1:
time: 451 us; the launch traced here: 450 us
  waiting for transfers between devices  309 us (69%)
  matrix products  57.7 us (13%)
  local copies, waits for them, and re-layouts  43.9 us (10%)
  other arithmetic  16.3 us (4%)
  between operations  13.9 us (3%)
  starting transfers between devices  8.72 us (2%)
    psum x1, waiting for transfers between devices, body(): summed = lax.psum(partial_both, 'row')  158 us
    reduce_scatter x1, waiting for transfers between devices, body(): lax.psum_scatter(jnp.dot(hidden, w_down, preferred_element_type=jnp.float...  87.6 us
    reduce_scatter x1, waiting for transfers between devices, body(): lax.psum_scatter(contract_last(dgate, w_gate) + contract_last(dup, w_up),...  36.1 us
    unnamed x23, local copies, waits for them, and re-layouts  31.7 us
    dot_general x3, matrix products, contract_first(): lax.dot_general(left, right, (((0,), (0,)), ((), ())), preferred_element_...  21 us
    dot_general x3, matrix products, contract_last(): lax.dot_general(left, right, (((1,), (1,)), ((), ())), preferred_element_...  15.7 us
    all_to_all x1, waiting for transfers between devices, body(): lax.all_to_all(jnp.stack([cotangent] * lax.axis_size('col')), 'col', 0, 0)  14.4 us
    all_gather x1, waiting for transfers between devices, body(): panel = lax.all_gather(tokens, 'col', axis=0, tiled=True)  12.5 us
  transfers between devices with their start and end apart: 5, of which 5 were waited for; matrix products, arithmetic and copies ran while one was open for 20% of the time, Pallas kernels for 0%

profile of v1, /device:TPU:0, one launch (start us, length us, event | category | flops | bytes accessed | tf_op | source)
XLA Modules:
  0.0 449.6 jit_solution(3770028686427340977)
XLA Ops:
  7.2 0.0 all-gather.2.cloned.1.call-start
  7.2 0.7 all-gather.2.cloned.1.call-update
  7.9 2.9 stack.2
  10.8 8.4 %all-to-all-start = ((bf16[32,24,2048]{2,1,0:T(8,128)(2,1)}), bf16[32,24,2048]{2,1,0:T(8,128)(2,1)S(1)}, u32[]{:S(2)}, u32[]{:S(2)}) async-start(bf16[32,24,2048]{2,1,0:T(8,128)(2,1)} %stack.2), calls=%async_computation.1 | async-start | bytes 6291456 | tf_op jit(solution)/shard_map/all_to_all | solution.py:54
  19.2 0.0 all-reduce.3.cloned.1.call-start
  19.3 0.0 copy-done.6
  19.3 0.1 broadcast_in_dim.18
  19.4 0.1 convert_element_type.67
  19.6 0.0 copy-done.7
  19.6 0.1 broadcast_in_dim.20
  19.7 0.1 convert_element_type.70
  19.9 6.1 %copy.24 = bf16[2048,896]{0,1:T(8,128)(2,1)} copy(bf16[2048,896]{1,0:T(8,128)(2,1)} %param.9) | data formatting | bytes 7340032 | tf_op args[1]
  25.9 6.1 %copy.25 = bf16[2048,896]{0,1:T(8,128)(2,1)} copy(bf16[2048,896]{1,0:T(8,128)(2,1)} %param.10) | data formatting | bytes 7340032 | tf_op args[2]
  32.0 0.0 copy-done.8
  32.0 0.1 copy.26
  32.1 0.1 broadcast_in_dim.22
  32.2 0.1 convert_element_type.74
  32.4 6.1 %copy.27 = bf16[896,2048]{0,1:T(8,128)(2,1)} copy(bf16[896,2048]{1,0:T(8,128)(2,1)} %param.11) | data formatting | bytes 7340032 | tf_op args[3]
  38.5 4.4 bitcast_multiply_fusion.4
  42.9 0.0 copy-done
  42.9 1.2 copy-done.1
  44.1 3.6 bitcast_multiply_fusion.2
  47.7 14.4 %all-to-all-done = bf16[32,24,2048]{2,1,0:T(8,128)(2,1)S(1)} async-done(((bf16[32,24,2048]{2,1,0:T(8,128)(2,1)}), bf16[32,24,2048]{2,1,0:T(8,128)(2,1)S(1)}, u32[]{:S(2)}, u32[]{:S(2)}) %all-to-all-start) | async-done | bytes 3145760 | tf_op jit(solution)/shard_map/all_to_all | solution.py:54
  62.1 6.7 %convolution_bitcast_fusion = f32[768,896]{0,1:T(8,128)} fusion(bf16[896,2048]{0,1:T(8,128)(2,1)} %bitcast_multiply_fusion.4, bf16[768,2048]{1,0:T(8,128)(2,1)S(1)} %bitcast.43), kind=kOutput, calls=%fused_computation.18 | convolution fusion | flops 2818572288 | bytes 9568256 | tf_op jit(solution)/shard_map/dot_general | solution.py:14
  68.8 12.5 %all-gather.2.cloned.1.call-done = bf16[768,2048]{1,0:T(8,128)(2,1)} async-done(((bf16[24,2048]{1,0:T(8,128)(2,1)}), bf16[768,2048]{1,0:T(8,128)(2,1)}) %all-gather.2.cloned.1.call-update) | async-done | bytes 3145744 | tf_op jit(solution)/shard_map/all_gather | solution.py:40
  81.3 12.4 %fusion.6 = f32[768,1792]{0,1:T(8,128)} fusion(bf16[768,2048]{1,0:T(8,128)(2,1)} %all-gather.2.cloned.1.call-done, bf16[2048,896]{0,1:T(8,128)(2,1)} %get-tuple-element.25, bf16[2048,896]{0,1:T(8,128)(2,1)} %get-tuple-element.26), kind=kOutput, calls=%fused_computation.11 | convolution fusion | flops 5651824640 | bytes 15990784 | tf_op jit(solution)/shard_map/dot_general | solution.py:42
  93.7 0.0 all-reduce.3.cloned.1.call-update
  93.7 0.2 reduce-scatter.5.cloned.1.call-start
  94.0 157.7 %all-reduce.3.cloned.1.call-done = (f32[768,1792]{0,1:T(8,128)}, f32[768,896]{0,1:T(8,128)}) async-done(((f32[768,1792]{0,1:T(8,128)}, f32[768,896]{0,1:T(8,128)}), (f32[768,1792]{0,1:T(8,128)}, f32[768,896]{0,1:T(8,128)})) %all-reduce.3.cloned.1.call-update) | async-done | bytes 8257552 | tf_op jit(solution)/shard_map/psum | solution.py:43
  251.7 5.1 %multiply_convert_fusion.1 = (bf16[768,896]{0,1:T(8,128)(2,1)S(1)}, bf16[768,896]{0,1:T(8,128)(2,1)S(1)}, bf16[768,896]{0,1:T(8,128)(2,1)}) fusion(f32[768,896]{0,1:T(8,128)} %get-tuple-element.21, f32[768,1792]{0,1:T(8,128)} %get-tuple-element.20), kind=kLoop, calls=%fused_computation.13 | loop fusion | flops 11010048 | bytes 12386304 | tf_op jit(solution)/shard_map/convert_element_type | solution.py:28
  256.8 0.0 copy-start.2
  256.8 3.5 fusion.11
  260.4 5.4 %convolution_add_fusion = f32[768,2048]{1,0:T(8,128)} fusion(f32[768,2048]{1,0:T(8,128)S(1)} %fusion.11, bf16[768,896]{0,1:T(8,128)(2,1)S(1)} %get-tuple-element.22, bf16[2048,896]{0,1:T(8,128)(2,1)S(1)} %copy-done.2), kind=kOutput, calls=%fused_computation.12 | convolution fusion | flops 2820145152 | bytes 17629184 | tf_op jit(solution)/shard_map/dot_general | solution.py:14
  265.8 0.0 reduce-scatter.5.cloned.1.call-update
  265.8 0.0 reduce-scatter.3.cloned.1.call-start
  265.9 8.6 %fusion.10 = f32[768,2048]{1,0:T(8,128)} fusion(bf16[768,896]{0,1:T(8,128)(2,1)} %get-tuple-element.24, bf16[896,2048]{0,1:T(8,128)(2,1)} %bitcast_multiply_fusion.4), kind=kOutput, calls=%fused_computation.20 | convolution fusion | flops 2818572288 | bytes 11337728 | tf_op jit(solution)/shard_map/dot_general | solution.py:48
  274.5 0.0 reduce-scatter.3.cloned.1.call-update
  274.5 2.1 broadcast_in_dim.23
  276.6 6.3 %copy.28 = bf16[896,2048]{1,0:T(8,128)(2,1)} copy(bf16[896,2048]{0,1:T(8,128)(2,1)} %bitcast.42) | data formatting | bytes 7340032 | tf_op jit(solution)/shard_map/convert_element_type | solution.py:10
  282.9 7.3 %fusion.5 = bf16[2048,896]{0,1:T(8,128)(2,1)} fusion(bf16[768,896]{0,1:T(8,128)(2,1)} %copy-done.5, bf16[768,2048]{1,0:T(8,128)(2,1)} %all-gather.2.cloned.1.call-done, bf16[2048,14]{0,1:T(8,128)(2,1)S(1)} %convert_element_type.67), kind=kOutput, calls=%fused_computation.7 | convolution fusion | flops 2824077312 | bytes 8249344 | tf_op jit(solution)/shard_map/dot_general | solution.py:20
  290.2 6.2 %copy.29 = bf16[2048,896]{1,0:T(8,128)(2,1)} copy(bf16[2048,896]{0,1:T(8,128)(2,1)} %fusion.5) | data formatting | bytes 7340032
  296.5 7.3 %fusion.4 = bf16[2048,896]{0,1:T(8,128)(2,1)} fusion(bf16[768,896]{0,1:T(8,128)(2,1)} %copy-done.4, bf16[768,2048]{1,0:T(8,128)(2,1)} %all-gather.2.cloned.1.call-done, bf16[2048,14]{0,1:T(8,128)(2,1)S(1)} %convert_element_type.70), kind=kOutput, calls=%fused_computation.5 | convolution fusion | flops 2824077312 | bytes 8249344 | tf_op jit(solution)/shard_map/dot_general | solution.py:20
  303.8 6.0 %copy.30 = bf16[2048,896]{1,0:T(8,128)(2,1)} copy(bf16[2048,896]{0,1:T(8,128)(2,1)} %fusion.4) | data formatting | bytes 7340032
  309.9 6.3 %multiply_convert_fusion = bf16[896,2048]{1,0:T(8,128)(2,1)} fusion(bf16[896,2048]{1,0:T(8,128)(2,1)} %copy.28, bf16[768,896]{0,1:T(8,128)(2,1)} %get-tuple-element.24, bf16[768,2048]{1,0:T(8,128)(2,1)S(1)} %bitcast.44), kind=kOutput, calls=%fused_computation.8 | convolution fusion | flops 2824077312 | bytes 11862016 | tf_op jit(solution)/shard_map/dot_general | solution.py:20
  316.2 36.1 %reduce-scatter.5.cloned.1.call-done = f32[24,2048]{1,0:T(8,128)} async-done(((f32[768,2048]{1,0:T(8,128)}), f32[24,2048]{1,0:T(8,128)}) %reduce-scatter.5.cloned.1.call-update) | async-done | bytes 196624 | tf_op jit(solution)/shard_map/reduce_scatter | solution.py:62
  352.3 1.6 convert_element_type.79
  353.8 87.6 %reduce-scatter.3.cloned.1.call-done = f32[24,2048]{1,0:T(8,128)} async-done(((f32[768,2048]{1,0:T(8,128)}), f32[24,2048]{1,0:T(8,128)}) %reduce-scatter.3.cloned.1.call-update) | async-done | bytes 196624 | tf_op jit(solution)/shard_map/reduce_scatter | solution.py:47
  441.5 1.6 convert_element_type.76
  (15 shorter events, 0.0 us)
Async XLA Ops:
  7.2 74.1 %all-gather.2.cloned.1.call-start = ((), (), s32[]{:S(2)}) async-start(), calls=%async_computation.3 | async-start | bytes 3244032 | tf_op jit(solution)/shard_map/all_gather | solution.py:40
  10.8 8.4 %copy-start.6 = (s32[32,14]{0,1:T(8,128)S(1)}, s32[32,14]{0,1:T(8,128)}, u32[]{:S(2)}) copy-start(s32[32,14]{0,1:T(8,128)} %param.12) | copy-start | bytes 5380
  10.8 8.7 %copy-start.7 = (s32[32,14]{0,1:T(8,128)S(1)}, s32[32,14]{0,1:T(8,128)}, u32[]{:S(2)}) copy-start(s32[32,14]{0,1:T(8,128)} %param.13) | copy-start | bytes 5380
  10.8 51.2 %all-to-all-start = ((bf16[32,24,2048]{2,1,0:T(8,128)(2,1)}), bf16[32,24,2048]{2,1,0:T(8,128)(2,1)S(1)}, u32[]{:S(2)}, u32[]{:S(2)}) async-start(bf16[32,24,2048]{2,1,0:T(8,128)(2,1)} %stack.2), calls=%async_computation.1 | async-start | bytes 6291456 | tf_op jit(solution)/shard_map/all_to_all | solution.py:54
  19.2 232.4 %all-reduce.3.cloned.1.call-start = ((), (), s32[]{:S(2)}) async-start(), calls=%async_computation.6 | async-start | bytes 16515072 | tf_op jit(solution)/shard_map/psum | solution.py:43
  25.9 6.1 %copy-start.8 = (s32[14,32]{1,0:T(8,128)S(1)}, s32[14,32]{1,0:T(8,128)}, u32[]{:S(2)}) copy-start(s32[14,32]{1,0:T(8,128)} %param.14) | copy-start | bytes 5380
  38.5 4.4 copy-start
  38.5 5.6 %copy-start.1 = (bf16[2048,896]{0,1:T(8,128)(2,1)S(1)}, bf16[2048,896]{0,1:T(8,128)(2,1)}, u32[]{:S(2)}) copy-start(bf16[2048,896]{0,1:T(8,128)(2,1)} %copy.25) | copy-start | bytes 11010052
  93.7 258.5 %reduce-scatter.5.cloned.1.call-start = ((), (), s32[]{:S(2)}) async-start(), calls=%async_computation.5 | async-start | bytes 6488064 | tf_op jit(solution)/shard_map/reduce_scatter | solution.py:62
  251.6 5.2 %copy-start.3 = (bf16[2048,896]{0,1:T(8,128)(2,1)S(1)}, bf16[2048,896]{0,1:T(8,128)(2,1)}, u32[]{:S(2)}) copy-start(bf16[2048,896]{0,1:T(8,128)(2,1)} %get-tuple-element.26) | copy-start | bytes 11010052
  256.8 3.6 copy-start.5
  256.8 3.6 copy-start.4
  256.8 3.6 copy-start.2
  265.8 175.6 %reduce-scatter.3.cloned.1.call-start = ((), (), s32[]{:S(2)}) async-start(), calls=%async_computation.4 | async-start | bytes 6488064 | tf_op jit(solution)/shard_map/reduce_scatter | solution.py:47
Sparse Core Ops, SparseCore 0:
  10.3 70.9 all-gather.1
  93.9 157.7 all-reduce.2
  266.0 86.2 reduce-scatter.4
  355.8 85.5 reduce-scatter.2
